TPU v7x, 256 devices: a whole 4x4x8 slice. The times are simulated.
256 devices in a mesh: grp: 8 (over y, core), dev: 32 (over z, x).
Axes of the slice: x: 4, y: 4, z: 8, core: 2. Of those that a mesh axis runs over, the one named last changes fastest.
Arguments:
- objective: float32 [8, 32, 1024, 256], P('grp', 'dev'), may hold values from -24 to 24
- schur: float32 [8, 32, 1024, 1024], P('grp', 'dev')
- local_inverse: float32 [8, 32, 1024, 1024], P('grp', 'dev')
- coarse_basis: float32 [8, 32, 64, 1024], P('grp', 'dev'), may hold values from -0.09375 to 0.09375
- coarse_inverse: float32 [8, 32, 32, 8192], P(None, 'dev', None, 'grp')
- stiffness: int32 [8, 32, 1024], P('grp', 'dev'), may hold values from 1 to 8
- face_rows: int32 [8, 32, 4, 256], P('grp', 'dev'), may hold values from -1 to 1023, as said below
- coarse_map: int32 [8, 32, 64], P('grp', 'dev'), may hold values from 0 to 255
Outputs:
- adjoint: float32 [8, 32, 1024, 256], P('grp', 'dev')
Inputs may be any that keep to these rules, and one draw needn't show every extreme that they name: `face_rows`: slot k of face p names the local row of the k-th row that the subdomain shares with its neighbour across face p, or -1; the live slots of a face come first, and the neighbour lists the same shared rows in the same order in its opposite face. The live slots of a subdomain name its rows 0 to n - 1 once each, n at most 1024, and at least one subdomain has all 1024 rows. Faces at the ends of the layout are empty; a face that joins two subdomains has 1 to 256 rows. `coarse_map`: entry e of subdomain (g, d) names the coarse dof (e // 32, d, e % 32), owned by the subdomain at grp index e // 32 of the same dev index.
All inputs are finite; a program needn't handle non-finite values.
Results may differ from a plain program's by a relative error of at most 0.0003.
Values sent between devices are 32-bit elements; how exact they have to be, the bound alone decides.
No kernel may reach another device: no remote copies, remote signals or barrier semaphores. Data moves between devices by JAX's collectives and lax.ppermute only.
A program may use at most 64 MiB of HBM per device.

v0:
```python
import jax
import jax.numpy as jnp
from jax import lax
from jax.sharding import PartitionSpec as P

INTERFACE = 1024
FACE_ROWS = 256
OWNED = 32
SWEEPS = 2


def padded(value, sides, width):
    for axis, dim in sides:
        size, length = (lax.axis_size(axis), value.shape[dim])
        up = [(i, (i + 1) % size) for i in range(size - 1)]
        down = [(j, i) for i, j in up]
        last = lax.slice_in_dim(value, length - width, length, axis=dim)
        initial = lax.slice_in_dim(value, 0, width, axis=dim)
        before = lax.ppermute(last, axis, up)
        after = lax.ppermute(initial, axis, down)
        value = jnp.concatenate([before, value, after], axis=dim)
    return value


def contract_first(left, right):
    return lax.dot_general(
        left,
        right,
        (((0,), (0,)), ((), ())),
        precision=lax.Precision.HIGHEST,
        preferred_element_type=jnp.float32,
    )


def on_device(
    objective, schur, local_inverse, coarse_basis, coarse_inverse, stiffness, face_rows, coarse_map
):
    highest = lax.Precision.HIGHEST
    schur_block = schur[0, 0]
    local_block = local_inverse[0, 0]
    basis_rows = coarse_basis[0, 0]
    inverse_tile = coarse_inverse.reshape(-1, coarse_inverse.shape[3])
    slot_rows = face_rows[0, 0]
    local_map = coarse_map[0, 0]
    gradient = objective[0, 0]
    slot_count = 4 * FACE_ROWS
    slot_index = jnp.where(slot_rows < 0, INTERFACE, slot_rows).reshape(-1)
    empty_map = jnp.full((INTERFACE,), slot_count, jnp.int32)
    inverse = empty_map.at[slot_index].set(jnp.arange(slot_count, dtype=jnp.int32), mode="drop")
    live_rows = (inverse < slot_count).astype(jnp.float32)[:, None]

    def neighbour(values):
        packed = jnp.take(values, slot_index, axis=0, mode="fill", fill_value=0)
        packed = packed.reshape(4, FACE_ROWS, values.shape[-1])
        packet = jnp.stack([jnp.stack([packed[2], packed[1]]), jnp.stack([packed[0], packed[3]])])
        extended = padded(packet, (("grp", 0), ("dev", 1)), 1)
        received = jnp.stack([extended[1, 0], extended[2, 3], extended[0, 2], extended[3, 1]])
        received = received.reshape(slot_count, values.shape[-1])
        return jnp.take(received, inverse, axis=0, mode="fill", fill_value=0)

    multiplicity = stiffness[0, 0].astype(jnp.float32)[:, None]
    weight = live_rows * multiplicity / (multiplicity + neighbour(multiplicity))
    column_rows = inverse_tile.shape[0]
    onehot = (local_map[:, None] == jnp.arange(column_rows, dtype=jnp.int32)[None, :]).astype(
        jnp.float32
    )
    dev_position = lax.axis_index("dev")
    adjoint = jnp.zeros(gradient.shape, jnp.float32)
    for sweep_index in range(SWEEPS):
        if sweep_index == 0:
            remain = gradient
        else:
            remain = gradient - contract_first(schur_block, adjoint)
        residual = live_rows * (remain + neighbour(remain))
        weighted = weight * residual
        local_terms = jnp.dot(
            basis_rows, weighted, precision=highest, preferred_element_type=jnp.float32
        )
        spread_terms = contract_first(onehot, local_terms)
        column_residual = lax.psum(spread_terms, "grp")
        partial_sums = contract_first(inverse_tile, column_residual)
        summed = lax.psum(partial_sums, "dev")
        owned_part = lax.dynamic_slice_in_dim(summed, dev_position * OWNED, OWNED, 0)
        column_solution = lax.all_gather(owned_part, "grp", axis=0, tiled=True)
        local_solution = jnp.dot(
            onehot, column_solution, precision=highest, preferred_element_type=jnp.float32
        )
        correction = contract_first(basis_rows, local_solution)
        update = weight * (contract_first(local_block, weighted) + correction)
        adjoint = adjoint + update + neighbour(update)
    return adjoint[None, None]


def solution(mesh):
    return jax.shard_map(
        on_device,
        mesh=mesh,
        in_specs=(
            P("grp", "dev", None, None),
            P("grp", "dev", None, None),
            P("grp", "dev", None, None),
            P("grp", "dev", None, None),
            P(None, "dev", None, "grp"),
            P("grp", "dev", None),
            P("grp", "dev", None, None),
            P("grp", "dev", None),
        ),
        out_specs=P("grp", "dev", None, None),
        check_vma=False,
    )
```

profile of v0, /device:TPU:14, one launch (start us, length us, event | category | flops | bytes accessed | tf_op | source)
XLA Modules:
  0.0 766.2 jit_solution(6774467022367490812)
XLA Ops:
  41.0 5.8 collective-permute-start.6
  55.4 15.2 %collective-permute-done.6 = f32[4,1,256,256]{3,2,1,0:T(8,128)} collective-permute-done((f32[4,1,256,256]{3,2,1,0:T(8,128)}, f32[4,1,256,256]{3,2,1,0:T(8,128)}, u32[]{:S(2)}, u32[]{:S(2)}) %collective-permute-start.6) | collective-permute-done | bytes 1048608 | tf_op jit(solution)/shard_map/ppermute | solution.py:19
  71.5 9.8 %collective-permute-done.7 = f32[4,1,256,256]{3,2,1,0:T(8,128)S(1)} collective-permute-done((f32[4,1,256,256]{3,2,1,0:T(8,128)S(1)}, f32[4,1,256,256]{3,2,1,0:T(8,128)S(1)}, u32[]{:S(2)}, u32[]{:S(2)}) %collective-permute-start.7) | collective-permute-done | bytes 1048608 | tf_op jit(solution)/shard_map/ppermute | solution.py:20
  81.4 4.7 gather_fusion.3
  90.1 66.4 %all-reduce.5.cloned.1.call-done = f32[256,256]{1,0:T(8,128)} async-done(((f32[256,256]{1,0:T(8,128)}), f32[256,256]{1,0:T(8,128)}) %all-reduce.5.cloned.1.call-update) | async-done | bytes 262160 | tf_op jit(solution)/shard_map/psum | solution.py:80
  159.5 150.0 %all-reduce.7.cloned.1.call-done = f32[1024,256]{0,1:T(8,128)} async-done(((f32[1024,256]{0,1:T(8,128)}), f32[1024,256]{0,1:T(8,128)}) %all-reduce.7.cloned.1.call-update) | async-done | bytes 1048592 | tf_op jit(solution)/shard_map/psum | solution.py:82
  311.2 13.3 %all_gather.6 = f32[256,256]{1,0:T(8,128)S(1)} all-gather(f32[32,256]{1,0:T(8,128)} %copy.36), channel_id=1, replica_groups=mesh['grp'=8,'dev'=32] {'grp'}, dimensions={0}, use_global_device_ids=true | all-gather | bytes 294912 | tf_op jit(solution)/shard_map/all_gather | solution.py:84
  326.4 6.9 fusion.12
  334.9 4.7 gather_fusion.4
  345.8 4.7 collective-permute-done.9
  360.6 19.8 %collective-permute-done.10 = f32[4,1,256,256]{3,2,1,0:T(8,128)S(1)} collective-permute-done((f32[4,1,256,256]{3,2,1,0:T(8,128)S(1)}, f32[4,1,256,256]{3,2,1,0:T(8,128)S(1)}, u32[]{:S(2)}, u32[]{:S(2)}) %collective-permute-start.10) | collective-permute-done | bytes 1048608 | tf_op jit(solution)/shard_map/ppermute | solution.py:19
  380.4 5.8 collective-permute-done.11
  386.4 4.7 gather_fusion.5
  393.6 6.4 fusion.27
  400.4 4.7 gather_fusion.6
  425.5 19.1 %collective-permute-done.14 = f32[4,1,256,256]{3,2,1,0:T(8,128)S(1)} collective-permute-done((f32[4,1,256,256]{3,2,1,0:T(8,128)S(1)}, f32[4,1,256,256]{3,2,1,0:T(8,128)S(1)}, u32[]{:S(2)}, u32[]{:S(2)}) %collective-permute-start.14) | collective-permute-done | bytes 1048608 | tf_op jit(solution)/shard_map/ppermute | solution.py:19
  448.7 4.7 gather_fusion.7
  457.3 62.6 %all-reduce.9.cloned.1.call-done = f32[256,256]{1,0:T(8,128)} async-done(((f32[256,256]{1,0:T(8,128)}), f32[256,256]{1,0:T(8,128)}) %all-reduce.9.cloned.1.call-update) | async-done | bytes 262160 | tf_op jit(solution)/shard_map/psum | solution.py:80
  523.0 149.5 %all-reduce.11.cloned.1.call-done = f32[1024,256]{0,1:T(8,128)} async-done(((f32[1024,256]{0,1:T(8,128)}), f32[1024,256]{0,1:T(8,128)}) %all-reduce.11.cloned.1.call-update) | async-done | bytes 1048592 | tf_op jit(solution)/shard_map/psum | solution.py:82
  674.1 13.1 %all_gather.7 = f32[256,256]{1,0:T(8,128)S(1)} all-gather(f32[32,256]{1,0:T(8,128)} %copy.41), channel_id=1, replica_groups=mesh['grp'=8,'dev'=32] {'grp'}, dimensions={0}, use_global_device_ids=true | all-gather | bytes 294912 | tf_op jit(solution)/shard_map/all_gather | solution.py:84
  689.2 6.9 fusion.21
  706.2 4.7 collective-permute-done.17
  721.1 19.8 %collective-permute-done.18 = f32[4,1,256,256]{3,2,1,0:T(8,128)S(1)} collective-permute-done((f32[4,1,256,256]{3,2,1,0:T(8,128)S(1)}, f32[4,1,256,256]{3,2,1,0:T(8,128)S(1)}, u32[]{:S(2)}, u32[]{:S(2)}) %collective-permute-start.18) | collective-permute-done | bytes 1048608 | tf_op jit(solution)/shard_map/ppermute | solution.py:19
  740.8 5.8 collective-permute-done.19
  (163 shorter events, 143.1 us)
Async XLA Ops:
  6.5 149.9 %all-reduce.5.cloned.1.call-start = ((), (), s32[]{:S(2)}) async-start(), calls=%async_computation | async-start | bytes 524288 | tf_op jit(solution)/shard_map/psum | solution.py:80
  12.6 19.6 %collective-permute-start.1 = (f32[1,2,256,1]{2,1,3,0:T(2,128)S(1)}, f32[1,2,256,1]{2,1,3,0:T(2,128)S(1)}, u32[]{:S(2)}, u32[]{:S(2)}) collective-permute-start(f32[1,2,256,1]{2,1,3,0:T(2,128)S(1)} %maximum_bitcast_fusion.9), channel_id=1, source_target_pairs={{32,0},{64,32},{96,64},{128,96},{160,128},{192,160},{224,192},{33,... | collective-permute-start | bytes 6152 | tf_op jit(solution)/shard_map/ppermute | solution.py:20
  14.5 17.7 %collective-permute-start = (f32[1,2,256,1]{2,1,3,0:T(2,128)S(1)}, f32[1,2,256,1]{2,1,3,0:T(2,128)S(1)}, u32[]{:S(2)}, u32[]{:S(2)}) collective-permute-start(f32[1,2,256,1]{2,1,3,0:T(2,128)S(1)} %maximum_bitcast_fusion.8), channel_id=1, source_target_pairs={{0,32},{32,64},{64,96},{96,128},{128,160},{160,192},{192,224},{1,3... | collective-permute-start | bytes 6152 | tf_op jit(solution)/shard_map/ppermute | solution.py:19
  21.6 16.6 %collective-permute-start.5 = (f32[1,2,256,256]{3,2,1,0:T(8,128)}, f32[1,2,256,256]{3,2,1,0:T(8,128)}, u32[]{:S(2)}, u32[]{:S(2)}) collective-permute-start(f32[1,2,256,256]{3,2,1,0:T(8,128)} %maximum_bitcast_fusion.1), channel_id=1, source_target_pairs={{32,0},{64,32},{96,64},{128,96},{160,128},{192,160},{224,192},{33,... | collective-permute-start | bytes 1572872 | tf_op jit(solution)/shard_map/ppermute | solution.py:20
  25.6 12.6 %collective-permute-start.4 = (f32[1,2,256,256]{3,2,1,0:T(8,128)}, f32[1,2,256,256]{3,2,1,0:T(8,128)}, u32[]{:S(2)}, u32[]{:S(2)}) collective-permute-start(f32[1,2,256,256]{3,2,1,0:T(8,128)} %maximum_bitcast_fusion), channel_id=1, source_target_pairs={{0,32},{32,64},{64,96},{96,128},{128,160},{160,192},{192,224},{1,3... | collective-permute-start | bytes 1572872 | tf_op jit(solution)/shard_map/ppermute | solution.py:19
  32.3 5.9 collective-permute-start.2
  36.0 10.8 %collective-permute-start.3 = (f32[4,1,256,1]{2,1,3,0:T(1,128)S(1)}, f32[4,1,256,1]{2,1,3,0:T(1,128)S(1)}, u32[]{:S(2)}, u32[]{:S(2)}) collective-permute-start(f32[4,1,256,1]{2,1,3,0:T(1,128)S(1)} %get-tuple-element.38), channel_id=1, source_target_pairs={{1,0},{2,1},{3,2},{4,3},{5,4},{6,5},{7,6},{8,7},{9,8},{10,9},{11,1... | collective-permute-start | bytes 12296 | tf_op jit(solution)/shard_map/ppermute | solution.py:20
  41.0 29.5 %collective-permute-start.6 = (f32[4,1,256,256]{3,2,1,0:T(8,128)}, f32[4,1,256,256]{3,2,1,0:T(8,128)}, u32[]{:S(2)}, u32[]{:S(2)}) collective-permute-start(f32[4,1,256,256]{3,2,1,0:T(8,128)} %get-tuple-element.19), channel_id=1, source_target_pairs={{0,1},{1,2},{2,3},{3,4},{4,5},{5,6},{6,7},{7,8},{8,9},{9,10},{10,1... | collective-permute-start | bytes 3145736 | tf_op jit(solution)/shard_map/ppermute | solution.py:19
  51.4 29.9 %collective-permute-start.7 = (f32[4,1,256,256]{3,2,1,0:T(8,128)S(1)}, f32[4,1,256,256]{3,2,1,0:T(8,128)S(1)}, u32[]{:S(2)}, u32[]{:S(2)}) collective-permute-start(f32[4,1,256,256]{3,2,1,0:T(8,128)S(1)} %get-tuple-element.20), channel_id=1, source_target_pairs={{1,0},{2,1},{3,2},{4,3},{5,4},{6,5},{7,6},{8,7},{9,8},{10,9},{11,1... | collective-permute-start | bytes 3145736 | tf_op jit(solution)/shard_map/ppermute | solution.py:20
  90.0 219.4 %all-reduce.7.cloned.1.call-start = ((), (), s32[]{:S(2)}) async-start(), calls=%async_computation.1 | async-start | bytes 2097152 | tf_op jit(solution)/shard_map/psum | solution.py:82
  159.4 360.6 %all-reduce.9.cloned.1.call-start = ((), (), s32[]{:S(2)}) async-start(), calls=%async_computation.2 | async-start | bytes 524288 | tf_op jit(solution)/shard_map/psum | solution.py:80
  341.1 9.4 %collective-permute-start.9 = (f32[1,2,256,256]{3,2,1,0:T(8,128)S(1)}, f32[1,2,256,256]{3,2,1,0:T(8,128)S(1)}, u32[]{:S(2)}, u32[]{:S(2)}) collective-permute-start(f32[1,2,256,256]{3,2,1,0:T(8,128)S(1)} %maximum_bitcast_fusion.3), channel_id=1, source_target_pairs={{32,0},{64,32},{96,64},{128,96},{160,128},{192,160},{224,192},{33,... | collective-permute-start | bytes 1572872 | tf_op jit(solution)/shard_map/ppermute | solution.py:20
  343.9 10.5 %collective-permute-start.8 = (f32[1,2,256,256]{3,2,1,0:T(8,128)S(1)}, f32[1,2,256,256]{3,2,1,0:T(8,128)S(1)}, u32[]{:S(2)}, u32[]{:S(2)}) collective-permute-start(f32[1,2,256,256]{3,2,1,0:T(8,128)S(1)} %maximum_bitcast_fusion.2), channel_id=1, source_target_pairs={{0,32},{32,64},{64,96},{96,128},{128,160},{160,192},{192,224},{1,3... | collective-permute-start | bytes 1572872 | tf_op jit(solution)/shard_map/ppermute | solution.py:19
  354.6 25.8 %collective-permute-start.10 = (f32[4,1,256,256]{3,2,1,0:T(8,128)S(1)}, f32[4,1,256,256]{3,2,1,0:T(8,128)S(1)}, u32[]{:S(2)}, u32[]{:S(2)}) collective-permute-start(f32[4,1,256,256]{3,2,1,0:T(8,128)S(1)} %get-tuple-element.17), channel_id=1, source_target_pairs={{0,1},{1,2},{2,3},{3,4},{4,5},{5,6},{6,7},{7,8},{8,9},{9,10},{10,1... | collective-permute-start | bytes 3145736 | tf_op jit(solution)/shard_map/ppermute | solution.py:19
  358.7 27.6 %collective-permute-start.11 = (f32[4,1,256,256]{3,2,1,0:T(8,128)S(1)}, f32[4,1,256,256]{3,2,1,0:T(8,128)S(1)}, u32[]{:S(2)}, u32[]{:S(2)}) collective-permute-start(f32[4,1,256,256]{3,2,1,0:T(8,128)S(1)} %get-tuple-element.18), channel_id=1, source_target_pairs={{1,0},{2,1},{3,2},{4,3},{5,4},{6,5},{7,6},{8,7},{9,8},{10,9},{11,1... | collective-permute-start | bytes 3145736 | tf_op jit(solution)/shard_map/ppermute | solution.py:20
  406.6 8.6 %collective-permute-start.13 = (f32[1,2,256,256]{3,2,1,0:T(8,128)S(1)}, f32[1,2,256,256]{3,2,1,0:T(8,128)S(1)}, u32[]{:S(2)}, u32[]{:S(2)}) collective-permute-start(f32[1,2,256,256]{3,2,1,0:T(8,128)S(1)} %maximum_bitcast_fusion.5), channel_id=1, source_target_pairs={{32,0},{64,32},{96,64},{128,96},{160,128},{192,160},{224,192},{33,... | collective-permute-start | bytes 1572872 | tf_op jit(solution)/shard_map/ppermute | solution.py:20
  408.6 10.5 %collective-permute-start.12 = (f32[1,2,256,256]{3,2,1,0:T(8,128)S(1)}, f32[1,2,256,256]{3,2,1,0:T(8,128)S(1)}, u32[]{:S(2)}, u32[]{:S(2)}) collective-permute-start(f32[1,2,256,256]{3,2,1,0:T(8,128)S(1)} %maximum_bitcast_fusion.4), channel_id=1, source_target_pairs={{0,32},{32,64},{64,96},{96,128},{128,160},{160,192},{192,224},{1,3... | collective-permute-start | bytes 1572872 | tf_op jit(solution)/shard_map/ppermute | solution.py:19
  419.3 25.3 %collective-permute-start.14 = (f32[4,1,256,256]{3,2,1,0:T(8,128)S(1)}, f32[4,1,256,256]{3,2,1,0:T(8,128)S(1)}, u32[]{:S(2)}, u32[]{:S(2)}) collective-permute-start(f32[4,1,256,256]{3,2,1,0:T(8,128)S(1)} %get-tuple-element.15), channel_id=1, source_target_pairs={{0,1},{1,2},{2,3},{3,4},{4,5},{5,6},{6,7},{7,8},{8,9},{9,10},{10,1... | collective-permute-start | bytes 3145736 | tf_op jit(solution)/shard_map/ppermute | solution.py:19
  421.3 27.4 %collective-permute-start.15 = (f32[4,1,256,256]{3,2,1,0:T(8,128)S(1)}, f32[4,1,256,256]{3,2,1,0:T(8,128)S(1)}, u32[]{:S(2)}, u32[]{:S(2)}) collective-permute-start(f32[4,1,256,256]{3,2,1,0:T(8,128)S(1)} %get-tuple-element.16), channel_id=1, source_target_pairs={{1,0},{2,1},{3,2},{4,3},{5,4},{6,5},{7,6},{8,7},{9,8},{10,9},{11,1... | collective-permute-start | bytes 3145736 | tf_op jit(solution)/shard_map/ppermute | solution.py:20
  457.3 215.2 %all-reduce.11.cloned.1.call-start = ((), (), s32[]{:S(2)}) async-start(), calls=%async_computation.3 | async-start | bytes 2097152 | tf_op jit(solution)/shard_map/psum | solution.py:82
  701.5 9.4 %collective-permute-start.17 = (f32[1,2,256,256]{3,2,1,0:T(8,128)S(1)}, f32[1,2,256,256]{3,2,1,0:T(8,128)S(1)}, u32[]{:S(2)}, u32[]{:S(2)}) collective-permute-start(f32[1,2,256,256]{3,2,1,0:T(8,128)S(1)} %maximum_bitcast_fusion.7), channel_id=1, source_target_pairs={{32,0},{64,32},{96,64},{128,96},{160,128},{192,160},{224,192},{33,... | collective-permute-start | bytes 1572872 | tf_op jit(solution)/shard_map/ppermute | solution.py:20
  704.3 10.5 %collective-permute-start.16 = (f32[1,2,256,256]{3,2,1,0:T(8,128)S(1)}, f32[1,2,256,256]{3,2,1,0:T(8,128)S(1)}, u32[]{:S(2)}, u32[]{:S(2)}) collective-permute-start(f32[1,2,256,256]{3,2,1,0:T(8,128)S(1)} %maximum_bitcast_fusion.6), channel_id=1, source_target_pairs={{0,32},{32,64},{64,96},{96,128},{128,160},{160,192},{192,224},{1,3... | collective-permute-start | bytes 1572872 | tf_op jit(solution)/shard_map/ppermute | solution.py:19
  715.0 25.8 %collective-permute-start.18 = (f32[4,1,256,256]{3,2,1,0:T(8,128)S(1)}, f32[4,1,256,256]{3,2,1,0:T(8,128)S(1)}, u32[]{:S(2)}, u32[]{:S(2)}) collective-permute-start(f32[4,1,256,256]{3,2,1,0:T(8,128)S(1)} %get-tuple-element.13), channel_id=1, source_target_pairs={{0,1},{1,2},{2,3},{3,4},{4,5},{5,6},{6,7},{7,8},{8,9},{9,10},{10,1... | collective-permute-start | bytes 3145736 | tf_op jit(solution)/shard_map/ppermute | solution.py:19
  719.1 27.6 %collective-permute-start.19 = (f32[4,1,256,256]{3,2,1,0:T(8,128)S(1)}, f32[4,1,256,256]{3,2,1,0:T(8,128)S(1)}, u32[]{:S(2)}, u32[]{:S(2)}) collective-permute-start(f32[4,1,256,256]{3,2,1,0:T(8,128)S(1)} %get-tuple-element.14), channel_id=1, source_target_pairs={{1,0},{2,1},{3,2},{4,3},{5,4},{6,5},{7,6},{8,7},{9,8},{10,9},{11,1... | collective-permute-start | bytes 3145736 | tf_op jit(solution)/shard_map/ppermute | solution.py:20
  (15 other events, 245.1 us)
Sparse Core Ops, SparseCore 0:
  90.1 66.2 all-reduce.4
  160.3 149.1 all-reduce.6
  457.4 62.5 all-reduce.8
  523.3 149.1 all-reduce.10
where the time goes:
time: 767 us; the launch traced here: 766 us
  waiting for transfers between devices  553 us (72%)
  local copies, waits for them, and re-layouts  72.2 us (9%)
  starting transfers between devices  54.6 us (7%)
  matrix products  34.6 us (5%)
  blocking collectives  26.3 us (3%)
  between operations  14 us (2%)
  other arithmetic  11.2 us (1%)
    psum x2, waiting for transfers between devices, on_device(): summed = lax.psum(partial_sums, 'dev')  300 us
    psum x2, waiting for transfers between devices, on_device(): column_residual = lax.psum(spread_terms, 'grp')  129 us
    ppermute x10, waiting for transfers between devices, padded(): before = lax.ppermute(last, axis, up)  85.5 us
    ppermute x10, waiting for transfers between devices, padded(): after = lax.ppermute(initial, axis, down)  39.2 us
    gather x9, local copies, waits for them, and re-layouts, neighbour(): return jnp.take(received, inverse, axis=0, mode='fill', fill_value=0)  31.6 us
    dot_general x9, matrix products, contract_first(): lax.dot_general(left, right, (((0,), (0,)), ((), ())), precision=lax.Prec...  30.5 us
    ppermute x10, starting transfers between devices, padded(): before = lax.ppermute(last, axis, up)  30.1 us
    all_gather x2, blocking collectives, on_device(): column_solution = lax.all_gather(owned_part, 'grp', axis=0, tiled=True)  26.3 us
  transfers between devices with their start and end apart: 24, of which 18 were waited for; matrix products, arithmetic and copies ran while one was open for 3% of the time, Pallas kernels for 0%

commit v1 on v0

--- a/solution.py
+++ b/solution.py
@@ -79,7 +79,8 @@
         spread_terms = contract_first(onehot, local_terms)
         column_residual = lax.psum(spread_terms, "grp")
         partial_sums = contract_first(inverse_tile, column_residual)
-        summed = lax.psum(partial_sums, "dev")
+        parts = lax.all_gather(partial_sums, "dev")
+        summed = jnp.sum(parts, axis=0)
         owned_part = lax.dynamic_slice_in_dim(summed, dev_position * OWNED, OWNED, 0)
         column_solution = lax.all_gather(owned_part, "grp", axis=0, tiled=True)
         local_solution = jnp.dot(

time: 767 us -> 1010 us (1.32)
  waiting for transfers between devices: 553 us -> 719 us
  local copies, waits for them, and re-layouts: 72.2 us -> 128 us
  other arithmetic: 11.2 us -> 26.3 us
    all_gather x0 -> x2, waiting for transfers between devices: none -> 466 us  [on_device(): parts = lax.all_gather(partial_sums, 'dev')]
    psum x2 -> x0, waiting for transfers between devices: 300 us -> none  [on_device(): summed = lax.psum(partial_sums, 'dev')]
    unnamed x33 -> x35, local copies, waits for them, and re-layouts: 1.18 us -> 58.7 us
    reduce_sum x0 -> x2, other arithmetic: none -> 15.1 us  [on_device(): summed = jnp.sum(parts, axis=0)]
  transfers between devices with their start and end apart: 24 -> 24, of which waited for: 18 -> 18; matrix products, arithmetic and copies ran while one was open for 3% -> 2% of each run, Pallas kernels for 0% -> 0%
where the time goes in v1:
time: 1010 us; the launch traced here: 1000 us
  waiting for transfers between devices  719 us (71%)
  local copies, waits for them, and re-layouts  128 us (13%)
  starting transfers between devices  54.4 us (5%)
  matrix products  34.6 us (3%)
  blocking collectives  26.8 us (3%)
  other arithmetic  26.3 us (3%)
  between operations  14.3 us (1%)
    all_gather x2, waiting for transfers between devices, on_device(): parts = lax.all_gather(partial_sums, 'dev')  466 us
    psum x2, waiting for transfers between devices, on_device(): column_residual = lax.psum(spread_terms, 'grp')  130 us
    ppermute x10, waiting for transfers between devices, padded(): before = lax.ppermute(last, axis, up)  85.7 us
    unnamed x35, local copies, waits for them, and re-layouts  58.7 us
    ppermute x10, waiting for transfers between devices, padded(): after = lax.ppermute(initial, axis, down)  38.2 us
    gather x9, local copies, waits for them, and re-layouts, neighbour(): return jnp.take(received, inverse, axis=0, mode='fill', fill_value=0)  31.6 us
    dot_general x9, matrix products, contract_first(): lax.dot_general(left, right, (((0,), (0,)), ((), ())), precision=lax.Prec...  30.5 us
    ppermute x10, starting transfers between devices, padded(): before = lax.ppermute(last, axis, up)  29.1 us
  transfers between devices with their start and end apart: 24, of which 18 were waited for; matrix products, arithmetic and copies ran while one was open for 2% of the time, Pallas kernels for 0%

profile of v1, /device:TPU:14, one launch (start us, length us, event | category | flops | bytes accessed | tf_op | source)
XLA Modules:
  0.0 1003.7 jit_solution(3274192261730357233)
XLA Ops:
  41.0 5.8 collective-permute-start.6
  55.4 15.2 %collective-permute-done.6 = f32[4,1,256,256]{3,2,1,0:T(8,128)} collective-permute-done((f32[4,1,256,256]{3,2,1,0:T(8,128)}, f32[4,1,256,256]{3,2,1,0:T(8,128)}, u32[]{:S(2)}, u32[]{:S(2)}) %collective-permute-start.6) | collective-permute-done | bytes 1048608 | tf_op jit(solution)/shard_map/ppermute | solution.py:19
  71.5 9.8 collective-permute-done.7
  81.4 4.7 gather_fusion.3
  90.1 66.4 %all-reduce.3.cloned.1.call-done = f32[256,256]{1,0:T(8,128)} async-done(((f32[256,256]{1,0:T(8,128)}), f32[256,256]{1,0:T(8,128)}) %all-reduce.3.cloned.1.call-update) | async-done | bytes 262160 | tf_op jit(solution)/shard_map/psum | solution.py:80
  159.5 232.8 %all-gather.5.cloned.1.call-done = f32[32768,256]{0,1:T(8,128)} async-done(((f32[1024,256]{0,1:T(8,128)}), f32[32768,256]{0,1:T(8,128)}) %all-gather.5.cloned.1.call-update) | async-done | bytes 33554448 | tf_op jit(solution)/shard_map/all_gather | solution.py:82
  392.3 28.8 %copy.60 = f32[32,8,32,1024]{3,2,1,0:T(8,128)S(1)} copy(f32[32,8,32,1024]{3,1,2,0:T(8,128)} %bitcast.219) | data formatting | bytes 67108864
  421.1 7.6 bitcast_reduce_fusion.1
  429.5 13.5 %all_gather.20 = f32[256,256]{1,0:T(8,128)S(1)} all-gather(f32[32,256]{1,0:T(8,128)} %copy.48), channel_id=1, replica_groups=mesh['grp'=8,'dev'=32] {'grp'}, dimensions={0}, use_global_device_ids=true | all-gather | bytes 294912 | tf_op jit(solution)/shard_map/all_gather | solution.py:85
  444.9 6.9 fusion.12
  464.3 4.7 collective-permute-done.9
  479.1 19.9 %collective-permute-done.10 = f32[4,1,256,256]{3,2,1,0:T(8,128)S(1)} collective-permute-done((f32[4,1,256,256]{3,2,1,0:T(8,128)S(1)}, f32[4,1,256,256]{3,2,1,0:T(8,128)S(1)}, u32[]{:S(2)}, u32[]{:S(2)}) %collective-permute-start.10) | collective-permute-done | bytes 1048608 | tf_op jit(solution)/shard_map/ppermute | solution.py:19
  499.0 5.3 collective-permute-done.11
  511.7 6.4 fusion.27
  543.5 19.2 %collective-permute-done.14 = f32[4,1,256,256]{3,2,1,0:T(8,128)S(1)} collective-permute-done((f32[4,1,256,256]{3,2,1,0:T(8,128)S(1)}, f32[4,1,256,256]{3,2,1,0:T(8,128)S(1)}, u32[]{:S(2)}, u32[]{:S(2)}) %collective-permute-start.14) | collective-permute-done | bytes 1048608 | tf_op jit(solution)/shard_map/ppermute | solution.py:19
  575.4 63.4 %all-reduce.5.cloned.1.call-done = f32[256,256]{1,0:T(8,128)} async-done(((f32[256,256]{1,0:T(8,128)}), f32[256,256]{1,0:T(8,128)}) %all-reduce.5.cloned.1.call-update) | async-done | bytes 262160 | tf_op jit(solution)/shard_map/psum | solution.py:80
  641.8 232.9 %all-gather.7.cloned.1.call-done = f32[32768,256]{0,1:T(8,128)} async-done(((f32[1024,256]{0,1:T(8,128)}), f32[32768,256]{0,1:T(8,128)}) %all-gather.7.cloned.1.call-update) | async-done | bytes 33554448 | tf_op jit(solution)/shard_map/all_gather | solution.py:82
  874.6 28.8 %copy.61 = f32[32,8,32,1024]{3,2,1,0:T(8,128)S(1)} copy(f32[32,8,32,1024]{3,1,2,0:T(8,128)} %bitcast.220) | data formatting | bytes 67108864
  903.4 7.6 bitcast_reduce_fusion
  911.7 13.3 %all_gather.23 = f32[256,256]{1,0:T(8,128)S(1)} all-gather(f32[32,256]{1,0:T(8,128)} %copy.53), channel_id=1, replica_groups=mesh['grp'=8,'dev'=32] {'grp'}, dimensions={0}, use_global_device_ids=true | all-gather | bytes 294912 | tf_op jit(solution)/shard_map/all_gather | solution.py:85
  927.0 7.0 fusion.21
  944.0 4.7 collective-permute-done.17
  958.8 19.9 %collective-permute-done.18 = f32[4,1,256,256]{3,2,1,0:T(8,128)S(1)} collective-permute-done((f32[4,1,256,256]{3,2,1,0:T(8,128)S(1)}, f32[4,1,256,256]{3,2,1,0:T(8,128)S(1)}, u32[]{:S(2)}, u32[]{:S(2)}) %collective-permute-start.18) | collective-permute-done | bytes 1048608 | tf_op jit(solution)/shard_map/ppermute | solution.py:19
  978.7 5.3 collective-permute-done.19
  (167 shorter events, 159.7 us)
Async XLA Ops:
  6.5 149.9 %all-reduce.3.cloned.1.call-start = ((), (), s32[]{:S(2)}) async-start(), calls=%async_computation | async-start | bytes 524288 | tf_op jit(solution)/shard_map/psum | solution.py:80
  12.6 19.6 %collective-permute-start.1 = (f32[1,2,256,1]{2,1,3,0:T(2,128)S(1)}, f32[1,2,256,1]{2,1,3,0:T(2,128)S(1)}, u32[]{:S(2)}, u32[]{:S(2)}) collective-permute-start(f32[1,2,256,1]{2,1,3,0:T(2,128)S(1)} %maximum_bitcast_fusion.9), channel_id=1, source_target_pairs={{32,0},{64,32},{96,64},{128,96},{160,128},{192,160},{224,192},{33,... | collective-permute-start | bytes 6152 | tf_op jit(solution)/shard_map/ppermute | solution.py:20
  14.5 17.7 %collective-permute-start = (f32[1,2,256,1]{2,1,3,0:T(2,128)S(1)}, f32[1,2,256,1]{2,1,3,0:T(2,128)S(1)}, u32[]{:S(2)}, u32[]{:S(2)}) collective-permute-start(f32[1,2,256,1]{2,1,3,0:T(2,128)S(1)} %maximum_bitcast_fusion.8), channel_id=1, source_target_pairs={{0,32},{32,64},{64,96},{96,128},{128,160},{160,192},{192,224},{1,3... | collective-permute-start | bytes 6152 | tf_op jit(solution)/shard_map/ppermute | solution.py:19
  21.6 16.6 %collective-permute-start.5 = (f32[1,2,256,256]{3,2,1,0:T(8,128)}, f32[1,2,256,256]{3,2,1,0:T(8,128)}, u32[]{:S(2)}, u32[]{:S(2)}) collective-permute-start(f32[1,2,256,256]{3,2,1,0:T(8,128)} %maximum_bitcast_fusion.1), channel_id=1, source_target_pairs={{32,0},{64,32},{96,64},{128,96},{160,128},{192,160},{224,192},{33,... | collective-permute-start | bytes 1572872 | tf_op jit(solution)/shard_map/ppermute | solution.py:20
  25.6 12.6 %collective-permute-start.4 = (f32[1,2,256,256]{3,2,1,0:T(8,128)}, f32[1,2,256,256]{3,2,1,0:T(8,128)}, u32[]{:S(2)}, u32[]{:S(2)}) collective-permute-start(f32[1,2,256,256]{3,2,1,0:T(8,128)} %maximum_bitcast_fusion), channel_id=1, source_target_pairs={{0,32},{32,64},{64,96},{96,128},{128,160},{160,192},{192,224},{1,3... | collective-permute-start | bytes 1572872 | tf_op jit(solution)/shard_map/ppermute | solution.py:19
  32.3 5.9 collective-permute-start.2
  36.0 10.8 %collective-permute-start.3 = (f32[4,1,256,1]{2,1,3,0:T(1,128)S(1)}, f32[4,1,256,1]{2,1,3,0:T(1,128)S(1)}, u32[]{:S(2)}, u32[]{:S(2)}) collective-permute-start(f32[4,1,256,1]{2,1,3,0:T(1,128)S(1)} %get-tuple-element.38), channel_id=1, source_target_pairs={{1,0},{2,1},{3,2},{4,3},{5,4},{6,5},{7,6},{8,7},{9,8},{10,9},{11,1... | collective-permute-start | bytes 12296 | tf_op jit(solution)/shard_map/ppermute | solution.py:20
  41.0 29.5 %collective-permute-start.6 = (f32[4,1,256,256]{3,2,1,0:T(8,128)}, f32[4,1,256,256]{3,2,1,0:T(8,128)}, u32[]{:S(2)}, u32[]{:S(2)}) collective-permute-start(f32[4,1,256,256]{3,2,1,0:T(8,128)} %get-tuple-element.19), channel_id=1, source_target_pairs={{0,1},{1,2},{2,3},{3,4},{4,5},{5,6},{6,7},{7,8},{8,9},{9,10},{10,1... | collective-permute-start | bytes 3145736 | tf_op jit(solution)/shard_map/ppermute | solution.py:19
  51.4 29.9 %collective-permute-start.7 = (f32[4,1,256,256]{3,2,1,0:T(8,128)S(1)}, f32[4,1,256,256]{3,2,1,0:T(8,128)S(1)}, u32[]{:S(2)}, u32[]{:S(2)}) collective-permute-start(f32[4,1,256,256]{3,2,1,0:T(8,128)S(1)} %get-tuple-element.20), channel_id=1, source_target_pairs={{1,0},{2,1},{3,2},{4,3},{5,4},{6,5},{7,6},{8,7},{9,8},{10,9},{11,1... | collective-permute-start | bytes 3145736 | tf_op jit(solution)/shard_map/ppermute | solution.py:20
  90.0 302.3 %all-gather.5.cloned.1.call-start = ((), (), s32[]{:S(2)}) async-start(), calls=%async_computation.2 | async-start | bytes 34603008 | tf_op jit(solution)/shard_map/all_gather | solution.py:82
  159.5 479.3 %all-reduce.5.cloned.1.call-start = ((), (), s32[]{:S(2)}) async-start(), calls=%async_computation.1 | async-start | bytes 524288 | tf_op jit(solution)/shard_map/psum | solution.py:80
  459.7 9.4 collective-permute-start.9
  462.4 10.5 %collective-permute-start.8 = (f32[1,2,256,256]{3,2,1,0:T(8,128)S(1)}, f32[1,2,256,256]{3,2,1,0:T(8,128)S(1)}, u32[]{:S(2)}, u32[]{:S(2)}) collective-permute-start(f32[1,2,256,256]{3,2,1,0:T(8,128)S(1)} %maximum_bitcast_fusion.2), channel_id=1, source_target_pairs={{0,32},{32,64},{64,96},{96,128},{128,160},{160,192},{192,224},{1,3... | collective-permute-start | bytes 1572872 | tf_op jit(solution)/shard_map/ppermute | solution.py:19
  473.2 25.8 %collective-permute-start.10 = (f32[4,1,256,256]{3,2,1,0:T(8,128)S(1)}, f32[4,1,256,256]{3,2,1,0:T(8,128)S(1)}, u32[]{:S(2)}, u32[]{:S(2)}) collective-permute-start(f32[4,1,256,256]{3,2,1,0:T(8,128)S(1)} %get-tuple-element.17), channel_id=1, source_target_pairs={{0,1},{1,2},{2,3},{3,4},{4,5},{5,6},{6,7},{7,8},{8,9},{9,10},{10,1... | collective-permute-start | bytes 3145736 | tf_op jit(solution)/shard_map/ppermute | solution.py:19
  476.7 27.6 %collective-permute-start.11 = (f32[4,1,256,256]{3,2,1,0:T(8,128)S(1)}, f32[4,1,256,256]{3,2,1,0:T(8,128)S(1)}, u32[]{:S(2)}, u32[]{:S(2)}) collective-permute-start(f32[4,1,256,256]{3,2,1,0:T(8,128)S(1)} %get-tuple-element.18), channel_id=1, source_target_pairs={{1,0},{2,1},{3,2},{4,3},{5,4},{6,5},{7,6},{8,7},{9,8},{10,9},{11,1... | collective-permute-start | bytes 3145736 | tf_op jit(solution)/shard_map/ppermute | solution.py:20
  524.7 8.6 collective-permute-start.13
  526.6 10.5 %collective-permute-start.12 = (f32[1,2,256,256]{3,2,1,0:T(8,128)S(1)}, f32[1,2,256,256]{3,2,1,0:T(8,128)S(1)}, u32[]{:S(2)}, u32[]{:S(2)}) collective-permute-start(f32[1,2,256,256]{3,2,1,0:T(8,128)S(1)} %maximum_bitcast_fusion.4), channel_id=1, source_target_pairs={{0,32},{32,64},{64,96},{96,128},{128,160},{160,192},{192,224},{1,3... | collective-permute-start | bytes 1572872 | tf_op jit(solution)/shard_map/ppermute | solution.py:19
  537.4 25.3 %collective-permute-start.14 = (f32[4,1,256,256]{3,2,1,0:T(8,128)S(1)}, f32[4,1,256,256]{3,2,1,0:T(8,128)S(1)}, u32[]{:S(2)}, u32[]{:S(2)}) collective-permute-start(f32[4,1,256,256]{3,2,1,0:T(8,128)S(1)} %get-tuple-element.15), channel_id=1, source_target_pairs={{0,1},{1,2},{2,3},{3,4},{4,5},{5,6},{6,7},{7,8},{8,9},{9,10},{10,1... | collective-permute-start | bytes 3145736 | tf_op jit(solution)/shard_map/ppermute | solution.py:19
  539.3 27.4 %collective-permute-start.15 = (f32[4,1,256,256]{3,2,1,0:T(8,128)S(1)}, f32[4,1,256,256]{3,2,1,0:T(8,128)S(1)}, u32[]{:S(2)}, u32[]{:S(2)}) collective-permute-start(f32[4,1,256,256]{3,2,1,0:T(8,128)S(1)} %get-tuple-element.16), channel_id=1, source_target_pairs={{1,0},{2,1},{3,2},{4,3},{5,4},{6,5},{7,6},{8,7},{9,8},{10,9},{11,1... | collective-permute-start | bytes 3145736 | tf_op jit(solution)/shard_map/ppermute | solution.py:20
  575.4 299.3 %all-gather.7.cloned.1.call-start = ((), (), s32[]{:S(2)}) async-start(), calls=%async_computation.3 | async-start | bytes 34603008 | tf_op jit(solution)/shard_map/all_gather | solution.py:82
  939.3 9.4 collective-permute-start.17
  942.1 10.5 %collective-permute-start.16 = (f32[1,2,256,256]{3,2,1,0:T(8,128)S(1)}, f32[1,2,256,256]{3,2,1,0:T(8,128)S(1)}, u32[]{:S(2)}, u32[]{:S(2)}) collective-permute-start(f32[1,2,256,256]{3,2,1,0:T(8,128)S(1)} %maximum_bitcast_fusion.6), channel_id=1, source_target_pairs={{0,32},{32,64},{64,96},{96,128},{128,160},{160,192},{192,224},{1,3... | collective-permute-start | bytes 1572872 | tf_op jit(solution)/shard_map/ppermute | solution.py:19
  952.9 25.8 %collective-permute-start.18 = (f32[4,1,256,256]{3,2,1,0:T(8,128)S(1)}, f32[4,1,256,256]{3,2,1,0:T(8,128)S(1)}, u32[]{:S(2)}, u32[]{:S(2)}) collective-permute-start(f32[4,1,256,256]{3,2,1,0:T(8,128)S(1)} %get-tuple-element.13), channel_id=1, source_target_pairs={{0,1},{1,2},{2,3},{3,4},{4,5},{5,6},{6,7},{7,8},{8,9},{9,10},{10,1... | collective-permute-start | bytes 3145736 | tf_op jit(solution)/shard_map/ppermute | solution.py:19
  956.4 27.6 %collective-permute-start.19 = (f32[4,1,256,256]{3,2,1,0:T(8,128)S(1)}, f32[4,1,256,256]{3,2,1,0:T(8,128)S(1)}, u32[]{:S(2)}, u32[]{:S(2)}) collective-permute-start(f32[4,1,256,256]{3,2,1,0:T(8,128)S(1)} %get-tuple-element.14), channel_id=1, source_target_pairs={{1,0},{2,1},{3,2},{4,3},{5,4},{6,5},{7,6},{8,7},{9,8},{10,9},{11,1... | collective-permute-start | bytes 3145736 | tf_op jit(solution)/shard_map/ppermute | solution.py:20
  (15 other events, 245.1 us)
Sparse Core Ops, SparseCore 0:
  90.1 66.2 all-reduce.2
  159.6 232.6 all-gather.4
  575.5 63.2 all-reduce.4
  641.9 232.6 all-gather.6
